TPU v7x, 32 devices: a whole 2x2x4 slice. The times are simulated.
32 devices in a mesh: cols: 16 (over z, y, x), params: 2 (over core).
Axes of the slice: x: 2, y: 2, z: 4, core: 2. Of those that a mesh axis runs over, the one named last changes fastest.
Arguments:
- concentration: float32 [128, 16384], P(None, ('cols', 'params')), may hold values from 0.2 to 5
- emissions: float32 [128, 16384], P(None, ('cols', 'params')), may hold values from 0 to 1
- rate_table: float32 [8, 16, 16], replicated, may hold values from 0.01 to 0.3
- species_order: int32 [128], replicated, may hold values from 0 to 127, each once
- sensitivity: float32 [4, 128, 32, 4, 128], P('params', None, 'cols'), may hold values from -6 to 6
- source_terms: bfloat16 [4, 128, 32, 4, 128], P('params', None, 'cols'), may hold values from 0 to 2
- courant_x: float32 [32, 4, 128], P('cols'), may hold values from 0.05 to 0.24
- upwind_x: int32 [32, 4, 128], P('cols'), may hold values from 0 to 1
- courant_y: float32 [32, 4, 128], P('cols'), may hold values from 0.05 to 0.24
- upwind_y: int32 [32, 4, 128], P('cols'), may hold values from 0 to 1
Outputs:
- new_concentration: float32 [128, 16384], P(None, ('cols', 'params'))
- new_sensitivity: float32 [4, 128, 32, 4, 128], P('params', None, 'cols')
- sensitivity_burden: float32 [4, 128], P('params')
- species_burden: float32 [128], replicated
Inputs may be any that keep to these rules, and one draw needn't show every extreme that they name: `species_order`: each species appears exactly once. `upwind_x`: 1 means the wind blows toward higher indices through the face. `upwind_y`: 1 means the wind blows toward higher indices through the face.
All inputs are finite; a program needn't handle non-finite values.
Results may differ from a plain program's by a relative error of at most 0.0016.
Values may be sent and summed in bfloat16 or wider, within the bound.
A program may use at most 128 MiB of HBM per device.

v0:
```python
import jax
import jax.numpy as jnp
from jax import lax
from jax.sharding import PartitionSpec as P

SUBSTEPS = 2


def for_sending(value):

    def short(part):
        return part.astype(jnp.bfloat16) if part.dtype == jnp.float32 else part

    return jax.tree.map(short, value)


def passed_along(value, axis, by):
    devices = lax.axis_size(axis)
    pairs = [(i, i + by) for i in range(devices) if 0 <= i + by < devices]
    return lax.ppermute(value, axis, pairs)


def invert_blocks(matrix):
    size = matrix.shape[1]
    positions = jnp.arange(size)

    def eliminate(pivot_index, current):
        pivot = 1.0 / current[:, pivot_index, pivot_index, :]
        pivot_row = current[:, pivot_index, :, :] * pivot[:, None, :]
        pivot_row = jnp.where(
            (positions == pivot_index)[None, :, None], pivot[:, None, :], pivot_row
        )
        column = current[:, :, pivot_index, :]
        updated = current - column[:, :, None, :] * pivot_row[:, None, :, :]
        updated = jnp.where(
            (positions == pivot_index)[None, None, :, None],
            -column[:, :, None, :] * pivot[:, None, None, :],
            updated,
        )
        updated = jnp.where(
            (positions == pivot_index)[None, :, None, None], pivot_row[:, None, :, :], updated
        )
        return updated

    return lax.fori_loop(0, size, eliminate, matrix)


def build_factors(conc_cells, species_order, rate_table):
    block_count, block_width = (rate_table.shape[0], rate_table.shape[1])
    ordered = jnp.take(conc_cells, species_order, axis=0).reshape(block_count, block_width, -1)
    coupling = rate_table[:, :, :, None] * ordered[:, None, :, :]
    row_total = jnp.sum(coupling, axis=2)
    positions = jnp.arange(block_width)
    identity = (positions[:, None] == positions[None, :]).astype(jnp.float32)
    system = identity[None, :, :, None] * (1.0 + row_total)[:, :, None, :] - coupling
    return invert_blocks(system).astype(jnp.bfloat16)


def apply_blocks(factors, values):
    result = jnp.zeros(values.shape, jnp.float32)
    for column_index in range(factors.shape[2]):
        result = (
            result
            + factors[:, :, column_index, :].astype(jnp.float32)[None]
            * values[:, :, column_index, :][:, :, None, :]
        )
    return result


def across_flux(tracer, courant_y, upwind_y):
    before_y = jnp.concatenate([jnp.zeros_like(tracer[..., :1]), tracer[..., :-1]], axis=4)
    lower_y = courant_y * jnp.where(upwind_y == 1, before_y, -tracer)
    upper_y = jnp.concatenate([lower_y[..., 1:], jnp.zeros_like(lower_y[..., :1])], axis=4)
    return lower_y - upper_y


def advect(tracer, courant_x, upwind_x, courant_y, upwind_y):
    left_plane = passed_along(for_sending(tracer[:, :, -1:]), "cols", 1)
    before_x = jnp.concatenate([left_plane, tracer[:, :, :-1]], axis=2)
    lower_x = courant_x * jnp.where(upwind_x == 1, before_x, -tracer)
    right_plane = passed_along(for_sending(lower_x[:, :, :1]), "cols", -1)
    upper_x = jnp.concatenate([lower_x[:, :, 1:], right_plane], axis=2)
    return tracer + lower_x - upper_x + across_flux(tracer, courant_y, upwind_y)


def shards(
    concentration,
    emissions,
    rate_table,
    species_order,
    sensitivity,
    source_terms,
    courant_x,
    upwind_x,
    courant_y,
    upwind_y,
):
    block_count, block_width = (rate_table.shape[0], rate_table.shape[1])
    groups, species = (sensitivity.shape[0], sensitivity.shape[1])
    planes, layers, across = (sensitivity.shape[2], sensitivity.shape[3], sensitivity.shape[4])
    cell_count = planes * layers * across
    inverse = jnp.argsort(species_order)
    own_factors = build_factors(concentration, species_order, rate_table)
    base_side = jnp.take(concentration + emissions, species_order, axis=0).reshape(
        block_count, block_width, -1
    )
    new_base = apply_blocks(own_factors, base_side[None])[0].reshape(species, -1)
    new_concentration = jnp.take(new_base, inverse, axis=0)
    tracer = sensitivity
    for substep in range(SUBSTEPS):
        tracer = advect(tracer, courant_x, upwind_x, courant_y, upwind_y)
    right_side = jnp.take(tracer + source_terms.astype(jnp.float32), species_order, axis=1)
    right_side = right_side.reshape(groups, block_count, block_width, cell_count)
    result = apply_blocks(lax.all_gather(own_factors, "params", axis=3, tiled=True), right_side)
    new_sensitivity = jnp.take(
        result.reshape(groups, species, planes, layers, across), inverse, axis=1
    )
    partial_sens = jnp.sum(new_sensitivity, axis=(2, 3, 4))
    partial_conc = jnp.sum(new_concentration, axis=1)
    total_cells = cell_count * lax.axis_size("cols")
    group_index = lax.axis_index("params")
    row_table = jnp.zeros((groups * lax.axis_size("params"), species), jnp.float32)
    row_table = lax.dynamic_update_slice(row_table, partial_sens, (group_index * groups, 0))
    table_total, conc_total = lax.psum((row_table, partial_conc), ("cols", "params"))
    sens_total = lax.dynamic_slice(table_total, (group_index * groups, 0), (groups, species))
    return (new_concentration, new_sensitivity, sens_total / total_cells, conc_total / total_cells)


def solution(mesh):
    in_specs = (
        P(None, ("cols", "params")),
        P(None, ("cols", "params")),
        P(),
        P(),
        P("params", None, "cols", None, None),
        P("params", None, "cols", None, None),
        P("cols", None, None),
        P("cols", None, None),
        P("cols", None, None),
        P("cols", None, None),
    )
    out_specs = (
        P(None, ("cols", "params")),
        P("params", None, "cols", None, None),
        P("params", None),
        P(),
    )
    return jax.shard_map(shards, mesh=mesh, in_specs=in_specs, out_specs=out_specs, check_vma=False)
```

profile of v0, /device:TPU:0, one launch (start us, length us, event | category | flops | bytes accessed | tf_op | source)
XLA Modules:
  0.0 349.7 jit_solution(16836673207462641334)
XLA Ops:
  11.6 2.5 sort.17
  15.8 2.5 multiply_subtract_fusion
  18.4 151.3 %while.14 = (s32[]{:T(128)}, f32[8,16,16,512]{3,2,1,0:T(8,128)}, s32[]{:T(128)}) while((s32[]{:T(128)}, f32[8,16,16,512]{3,2,1,0:T(8,128)}, s32[]{:T(128)}) %tuple.112), condition=%wide.region_2.4_spmd.clone, body=%wide.region_1.3_spmd.clone.sunk | while | flops 4460562 | bytes 11632757 | solution.py:45
  19.3 2.0 negate_multiply_fusion.2
  22.5 5.3 %select_select_fusion.2 = f32[8,16,16,512]{3,2,1,0:T(8,128)} fusion(f32[8,16,16,512]{3,2,1,0:T(8,128)} %get-tuple-element.200, f32[8,16,512]{2,1,0:T(8,128)S(1)} %get-tuple-element.194, f32[8,16,512]{2,1,0:T(8,128)S(1)} %get-tuple-element.195, f32[8,16,512]{2,1,0:T(8,128)S(1)} %select_bitcast_fusion.5, pred[16]{0:T(512)(128)(4,1)S(1)} %iota_compare_fusion.3), kind=kLoop, calls=%fused_computation.6.clone.1 | loop fusion | flops 4194304 | bytes 9175056 | tf_op jit(solution)/shard_map/while/body/eval_jaxpr/jit(_where)/select_n | solution.py:40
  28.8 2.0 negate_multiply_fusion.2
  31.9 5.3 %select_select_fusion.2 = f32[8,16,16,512]{3,2,1,0:T(8,128)} fusion(f32[8,16,16,512]{3,2,1,0:T(8,128)} %get-tuple-element.200, f32[8,16,512]{2,1,0:T(8,128)S(1)} %get-tuple-element.194, f32[8,16,512]{2,1,0:T(8,128)S(1)} %get-tuple-element.195, f32[8,16,512]{2,1,0:T(8,128)S(1)} %select_bitcast_fusion.5, pred[16]{0:T(512)(128)(4,1)S(1)} %iota_compare_fusion.3), kind=kLoop, calls=%fused_computation.6.clone.1 | loop fusion | flops 4194304 | bytes 9175056 | tf_op jit(solution)/shard_map/while/body/eval_jaxpr/jit(_where)/select_n | solution.py:40
  38.2 2.0 negate_multiply_fusion.2
  41.4 5.3 %select_select_fusion.2 = f32[8,16,16,512]{3,2,1,0:T(8,128)} fusion(f32[8,16,16,512]{3,2,1,0:T(8,128)} %get-tuple-element.200, f32[8,16,512]{2,1,0:T(8,128)S(1)} %get-tuple-element.194, f32[8,16,512]{2,1,0:T(8,128)S(1)} %get-tuple-element.195, f32[8,16,512]{2,1,0:T(8,128)S(1)} %select_bitcast_fusion.5, pred[16]{0:T(512)(128)(4,1)S(1)} %iota_compare_fusion.3), kind=kLoop, calls=%fused_computation.6.clone.1 | loop fusion | flops 4194304 | bytes 9175056 | tf_op jit(solution)/shard_map/while/body/eval_jaxpr/jit(_where)/select_n | solution.py:40
  47.7 2.0 negate_multiply_fusion.2
  50.8 5.3 %select_select_fusion.2 = f32[8,16,16,512]{3,2,1,0:T(8,128)} fusion(f32[8,16,16,512]{3,2,1,0:T(8,128)} %get-tuple-element.200, f32[8,16,512]{2,1,0:T(8,128)S(1)} %get-tuple-element.194, f32[8,16,512]{2,1,0:T(8,128)S(1)} %get-tuple-element.195, f32[8,16,512]{2,1,0:T(8,128)S(1)} %select_bitcast_fusion.5, pred[16]{0:T(512)(128)(4,1)S(1)} %iota_compare_fusion.3), kind=kLoop, calls=%fused_computation.6.clone.1 | loop fusion | flops 4194304 | bytes 9175056 | tf_op jit(solution)/shard_map/while/body/eval_jaxpr/jit(_where)/select_n | solution.py:40
  57.1 2.0 negate_multiply_fusion.2
  60.3 5.3 %select_select_fusion.2 = f32[8,16,16,512]{3,2,1,0:T(8,128)} fusion(f32[8,16,16,512]{3,2,1,0:T(8,128)} %get-tuple-element.200, f32[8,16,512]{2,1,0:T(8,128)S(1)} %get-tuple-element.194, f32[8,16,512]{2,1,0:T(8,128)S(1)} %get-tuple-element.195, f32[8,16,512]{2,1,0:T(8,128)S(1)} %select_bitcast_fusion.5, pred[16]{0:T(512)(128)(4,1)S(1)} %iota_compare_fusion.3), kind=kLoop, calls=%fused_computation.6.clone.1 | loop fusion | flops 4194304 | bytes 9175056 | tf_op jit(solution)/shard_map/while/body/eval_jaxpr/jit(_where)/select_n | solution.py:40
  66.6 2.0 negate_multiply_fusion.2
  69.8 5.3 %select_select_fusion.2 = f32[8,16,16,512]{3,2,1,0:T(8,128)} fusion(f32[8,16,16,512]{3,2,1,0:T(8,128)} %get-tuple-element.200, f32[8,16,512]{2,1,0:T(8,128)S(1)} %get-tuple-element.194, f32[8,16,512]{2,1,0:T(8,128)S(1)} %get-tuple-element.195, f32[8,16,512]{2,1,0:T(8,128)S(1)} %select_bitcast_fusion.5, pred[16]{0:T(512)(128)(4,1)S(1)} %iota_compare_fusion.3), kind=kLoop, calls=%fused_computation.6.clone.1 | loop fusion | flops 4194304 | bytes 9175056 | tf_op jit(solution)/shard_map/while/body/eval_jaxpr/jit(_where)/select_n | solution.py:40
  76.0 2.0 negate_multiply_fusion.2
  79.2 5.3 %select_select_fusion.2 = f32[8,16,16,512]{3,2,1,0:T(8,128)} fusion(f32[8,16,16,512]{3,2,1,0:T(8,128)} %get-tuple-element.200, f32[8,16,512]{2,1,0:T(8,128)S(1)} %get-tuple-element.194, f32[8,16,512]{2,1,0:T(8,128)S(1)} %get-tuple-element.195, f32[8,16,512]{2,1,0:T(8,128)S(1)} %select_bitcast_fusion.5, pred[16]{0:T(512)(128)(4,1)S(1)} %iota_compare_fusion.3), kind=kLoop, calls=%fused_computation.6.clone.1 | loop fusion | flops 4194304 | bytes 9175056 | tf_op jit(solution)/shard_map/while/body/eval_jaxpr/jit(_where)/select_n | solution.py:40
  85.5 2.0 negate_multiply_fusion.2
  88.7 5.3 %select_select_fusion.2 = f32[8,16,16,512]{3,2,1,0:T(8,128)} fusion(f32[8,16,16,512]{3,2,1,0:T(8,128)} %get-tuple-element.200, f32[8,16,512]{2,1,0:T(8,128)S(1)} %get-tuple-element.194, f32[8,16,512]{2,1,0:T(8,128)S(1)} %get-tuple-element.195, f32[8,16,512]{2,1,0:T(8,128)S(1)} %select_bitcast_fusion.5, pred[16]{0:T(512)(128)(4,1)S(1)} %iota_compare_fusion.3), kind=kLoop, calls=%fused_computation.6.clone.1 | loop fusion | flops 4194304 | bytes 9175056 | tf_op jit(solution)/shard_map/while/body/eval_jaxpr/jit(_where)/select_n | solution.py:40
  95.0 2.0 negate_multiply_fusion.2
  98.1 5.3 %select_select_fusion.2 = f32[8,16,16,512]{3,2,1,0:T(8,128)} fusion(f32[8,16,16,512]{3,2,1,0:T(8,128)} %get-tuple-element.200, f32[8,16,512]{2,1,0:T(8,128)S(1)} %get-tuple-element.194, f32[8,16,512]{2,1,0:T(8,128)S(1)} %get-tuple-element.195, f32[8,16,512]{2,1,0:T(8,128)S(1)} %select_bitcast_fusion.5, pred[16]{0:T(512)(128)(4,1)S(1)} %iota_compare_fusion.3), kind=kLoop, calls=%fused_computation.6.clone.1 | loop fusion | flops 4194304 | bytes 9175056 | tf_op jit(solution)/shard_map/while/body/eval_jaxpr/jit(_where)/select_n | solution.py:40
  104.4 2.0 negate_multiply_fusion.2
  107.6 5.3 %select_select_fusion.2 = f32[8,16,16,512]{3,2,1,0:T(8,128)} fusion(f32[8,16,16,512]{3,2,1,0:T(8,128)} %get-tuple-element.200, f32[8,16,512]{2,1,0:T(8,128)S(1)} %get-tuple-element.194, f32[8,16,512]{2,1,0:T(8,128)S(1)} %get-tuple-element.195, f32[8,16,512]{2,1,0:T(8,128)S(1)} %select_bitcast_fusion.5, pred[16]{0:T(512)(128)(4,1)S(1)} %iota_compare_fusion.3), kind=kLoop, calls=%fused_computation.6.clone.1 | loop fusion | flops 4194304 | bytes 9175056 | tf_op jit(solution)/shard_map/while/body/eval_jaxpr/jit(_where)/select_n | solution.py:40
  113.9 2.0 negate_multiply_fusion.2
  117.0 5.3 %select_select_fusion.2 = f32[8,16,16,512]{3,2,1,0:T(8,128)} fusion(f32[8,16,16,512]{3,2,1,0:T(8,128)} %get-tuple-element.200, f32[8,16,512]{2,1,0:T(8,128)S(1)} %get-tuple-element.194, f32[8,16,512]{2,1,0:T(8,128)S(1)} %get-tuple-element.195, f32[8,16,512]{2,1,0:T(8,128)S(1)} %select_bitcast_fusion.5, pred[16]{0:T(512)(128)(4,1)S(1)} %iota_compare_fusion.3), kind=kLoop, calls=%fused_computation.6.clone.1 | loop fusion | flops 4194304 | bytes 9175056 | tf_op jit(solution)/shard_map/while/body/eval_jaxpr/jit(_where)/select_n | solution.py:40
  123.3 2.0 negate_multiply_fusion.2
  126.5 5.3 %select_select_fusion.2 = f32[8,16,16,512]{3,2,1,0:T(8,128)} fusion(f32[8,16,16,512]{3,2,1,0:T(8,128)} %get-tuple-element.200, f32[8,16,512]{2,1,0:T(8,128)S(1)} %get-tuple-element.194, f32[8,16,512]{2,1,0:T(8,128)S(1)} %get-tuple-element.195, f32[8,16,512]{2,1,0:T(8,128)S(1)} %select_bitcast_fusion.5, pred[16]{0:T(512)(128)(4,1)S(1)} %iota_compare_fusion.3), kind=kLoop, calls=%fused_computation.6.clone.1 | loop fusion | flops 4194304 | bytes 9175056 | tf_op jit(solution)/shard_map/while/body/eval_jaxpr/jit(_where)/select_n | solution.py:40
  132.8 2.0 negate_multiply_fusion.2
  135.9 5.3 %select_select_fusion.2 = f32[8,16,16,512]{3,2,1,0:T(8,128)} fusion(f32[8,16,16,512]{3,2,1,0:T(8,128)} %get-tuple-element.200, f32[8,16,512]{2,1,0:T(8,128)S(1)} %get-tuple-element.194, f32[8,16,512]{2,1,0:T(8,128)S(1)} %get-tuple-element.195, f32[8,16,512]{2,1,0:T(8,128)S(1)} %select_bitcast_fusion.5, pred[16]{0:T(512)(128)(4,1)S(1)} %iota_compare_fusion.3), kind=kLoop, calls=%fused_computation.6.clone.1 | loop fusion | flops 4194304 | bytes 9175056 | tf_op jit(solution)/shard_map/while/body/eval_jaxpr/jit(_where)/select_n | solution.py:40
  142.2 2.0 negate_multiply_fusion.2
  145.4 5.3 %select_select_fusion.2 = f32[8,16,16,512]{3,2,1,0:T(8,128)} fusion(f32[8,16,16,512]{3,2,1,0:T(8,128)} %get-tuple-element.200, f32[8,16,512]{2,1,0:T(8,128)S(1)} %get-tuple-element.194, f32[8,16,512]{2,1,0:T(8,128)S(1)} %get-tuple-element.195, f32[8,16,512]{2,1,0:T(8,128)S(1)} %select_bitcast_fusion.5, pred[16]{0:T(512)(128)(4,1)S(1)} %iota_compare_fusion.3), kind=kLoop, calls=%fused_computation.6.clone.1 | loop fusion | flops 4194304 | bytes 9175056 | tf_op jit(solution)/shard_map/while/body/eval_jaxpr/jit(_where)/select_n | solution.py:40
  151.7 2.0 negate_multiply_fusion.2
  154.8 5.3 %select_select_fusion.2 = f32[8,16,16,512]{3,2,1,0:T(8,128)} fusion(f32[8,16,16,512]{3,2,1,0:T(8,128)} %get-tuple-element.200, f32[8,16,512]{2,1,0:T(8,128)S(1)} %get-tuple-element.194, f32[8,16,512]{2,1,0:T(8,128)S(1)} %get-tuple-element.195, f32[8,16,512]{2,1,0:T(8,128)S(1)} %select_bitcast_fusion.5, pred[16]{0:T(512)(128)(4,1)S(1)} %iota_compare_fusion.3), kind=kLoop, calls=%fused_computation.6.clone.1 | loop fusion | flops 4194304 | bytes 9175056 | tf_op jit(solution)/shard_map/while/body/eval_jaxpr/jit(_where)/select_n | solution.py:40
  161.1 2.0 negate_multiply_fusion.2
  164.3 5.3 %select_select_fusion.2 = f32[8,16,16,512]{3,2,1,0:T(8,128)} fusion(f32[8,16,16,512]{3,2,1,0:T(8,128)} %get-tuple-element.200, f32[8,16,512]{2,1,0:T(8,128)S(1)} %get-tuple-element.194, f32[8,16,512]{2,1,0:T(8,128)S(1)} %get-tuple-element.195, f32[8,16,512]{2,1,0:T(8,128)S(1)} %select_bitcast_fusion.5, pred[16]{0:T(512)(128)(4,1)S(1)} %iota_compare_fusion.3), kind=kLoop, calls=%fused_computation.6.clone.1 | loop fusion | flops 4194304 | bytes 9175056 | tf_op jit(solution)/shard_map/while/body/eval_jaxpr/jit(_where)/select_n | solution.py:40
  169.7 3.9 %convert_element_type.318 = bf16[8,16,16,512]{3,2,1,0:T(8,128)(2,1)} convert(f32[8,16,16,512]{3,2,1,0:T(8,128)} %get-tuple-element.71) | non-fusion elementwise | flops 1048576 | bytes 6291456 | tf_op jit(solution)/shard_map/convert_element_type | solution.py:56
  173.7 5.0 %collective-permute-start = (bf16[2,128,1,4,128]{4,3,2,1,0:T(4,128)(2,1)S(1)}, bf16[2,128,1,4,128]{4,3,2,1,0:T(4,128)(2,1)S(1)}, u32[]{:S(2)}, u32[]{:S(2)}) collective-permute-start(bf16[2,128,1,4,128]{4,3,2,1,0:T(4,128)(2,1)S(1)} %slice.447), channel_id=1, source_target_pairs={{0,2},{2,4},{4,6},{6,8},{8,10},{10,12},{12,14},{14,16},{16,18},{18... | collective-permute-start | bytes 786440 | tf_op jit(solution)/shard_map/ppermute | solution.py:20
  178.9 5.4 %collective-permute-done = bf16[2,128,1,4,128]{4,3,2,1,0:T(4,128)(2,1)S(1)} collective-permute-done((bf16[2,128,1,4,128]{4,3,2,1,0:T(4,128)(2,1)S(1)}, bf16[2,128,1,4,128]{4,3,2,1,0:T(4,128)(2,1)S(1)}, u32[]{:S(2)}, u32[]{:S(2)}) %collective-permute-start) | collective-permute-done | bytes 262176 | tf_op jit(solution)/shard_map/ppermute | solution.py:20
  186.7 4.4 %slice_convert_fusion.35 = (f32[8,16,1,512]{3,2,1,0:T(1,128)S(1)}, f32[8,16,1,512]{3,2,1,0:T(1,128)S(1)}, f32[8,16,1,512]{3,2,1,0:T(1,128)S(1)}, f32[8,16,1,512]...) fusion(bf16[8,16,16,512]{3,2,1,0:T(8,128)(2,1)S(1)} %copy-done), kind=kLoop, calls=%fused_computation.66 | loop fusion | flops 1048576 | bytes 6291456 | tf_op jit(solution)/shard_map/convert_element_type | solution.py:64
  191.8 3.4 collective-permute-done.1
  196.1 4.6 %collective-permute-start.2 = (bf16[2,128,1,4,128]{4,3,2,1,0:T(4,128)(2,1)S(1)}, bf16[2,128,1,4,128]{4,3,2,1,0:T(4,128)(2,1)S(1)}, u32[]{:S(2)}, u32[]{:S(2)}) collective-permute-start(bf16[2,128,1,4,128]{4,3,2,1,0:T(4,128)(2,1)S(1)} %slice.445), channel_id=1, source_target_pairs={{0,2},{2,4},{4,6},{6,8},{8,10},{10,12},{12,14},{14,16},{16,18},{18... | collective-permute-start | bytes 786440 | tf_op jit(solution)/shard_map/ppermute | solution.py:20
  201.0 3.5 %collective-permute-done.2 = bf16[2,128,1,4,128]{4,3,2,1,0:T(4,128)(2,1)S(1)} collective-permute-done((bf16[2,128,1,4,128]{4,3,2,1,0:T(4,128)(2,1)S(1)}, bf16[2,128,1,4,128]{4,3,2,1,0:T(4,128)(2,1)S(1)}, u32[]{:S(2)}, u32[]{:S(2)}) %collective-permute-start.2) | collective-permute-done | bytes 262176 | tf_op jit(solution)/shard_map/ppermute | solution.py:20
  224.3 2.8 fusion.7
  232.2 1.9 fusion.6
  234.1 2.6 gather_fusion.3
  269.6 18.6 %slice_convert_fusion.19 = (f32[8,16,1,1024]{3,2,1,0:T(1,128)}, f32[8,16,1,1024]{3,2,1,0:T(1,128)}, f32[8,16,1,1024]{3,2,1,0:T(1,128)}, f32[8,16,1,1024]{3,2,1,0...) fusion(bf16[8,16,16,1024]{3,2,1,0:T(8,128)(2,1)} %all-gather.2., ...), kind=kLoop, calls=%fused_computation.50 | loop fusion | flops 2097152 | bytes 12582912 | tf_op jit(solution)/shard_map/convert_element_type | solution.py:64
  288.3 5.7 %multiply_add_fusion = f32[2,128,1,8,128]{4,3,2,1,0:T(8,128)S(1)} fusion(f32[2,128,1,8,128]{4,3,2,1,0:T(8,128)S(1)} %bitcast.314, f32[2,128,1,8,128]{4,3,2,1,0:T(8,128)S(1)} %bitcast.315, f32[2,128,1,8,128]{4,3,2,1,0:T(8,128)S(1)} %bitcast.316, f32[2,128,1,8,128]{4,3,2,1,0:T(8,128)S(1)} %bitcast.317, f32[2,128,1,8,128]{4,3,2,1,0:T(8,128)S(1)} %bitcast.318, ...), kind=kLoop, calls=%fused_computation.28 | loop fusion | flops 8126464 | bytes 26214400 | tf_op jit(solution)/shard_map/add | solution.py:63
  297.4 44.4 %all-reduce.4 = (f32[4,128]{1,0:T(4,128)S(1)}, f32[128]{0:T(128)S(1)}) all-reduce(f32[4,128]{1,0:T(4,128)S(1)} %constant_dynamic-update-slice_fusion, f32[128]{0:T(128)S(1)} %get-tuple-element.95), channel_id=1, replica_groups=mesh['cols'=16,'params'=2] {'cols','params'}, use_global_device_ids=true, to_apply=%region_5.8 | all-reduce | flops 640 | bytes 5120 | tf_op jit(solution)/shard_map/psum | solution.py:124
  (255 shorter events, 104.8 us)
Async XLA Ops:
  7.2 4.4 %copy-start.21 = (s32[128]{0:T(128)S(1)}, s32[128]{0:T(128)}, u32[]{:S(2)}) copy-start(s32[128]{0:T(128)} %param.19) | copy-start | bytes 1540
  7.2 7.6 %copy-start.12 = (f32[8,16,16]{2,1,0:T(8,128)S(1)}, f32[8,16,16]{2,1,0:T(8,128)}, u32[]{:S(2)}) copy-start(f32[8,16,16]{2,1,0:T(8,128)} %param.18) | copy-start | bytes 24580
  7.2 262.3 %all-gather.2.cloned.1.call-start = ((), (), s32[]{:S(2)}) async-start(), calls=%async_computation | async-start | bytes 6291456 | tf_op jit(solution)/shard_map/all_gather | solution.py:114
  7.9 10.5 %copy-start.15 = (s32[1024]{0:T(1024)}, s32[1024]{0:T(1024)S(1)}, u32[]{:S(2)}) copy-start(s32[1024]{0:T(1024)S(1)} %pad_clamp_fusion.1) | copy-start | bytes 12292
  14.6 3.7 %copy-start.16 = (pred[128]{0:T(512)(128)(4,1)}, pred[128]{0:T(512)(128)(4,1)S(1)}, u32[]{:S(2)}) copy-start(pred[128]{0:T(512)(128)(4,1)S(1)} %get-tuple-element.172) | copy-start | bytes 388
  169.6 4.0 %copy-start.1 = (f32[2,128,2,4,128]{4,3,2,1,0:T(4,128)S(1)}, f32[2,128,2,4,128]{4,3,2,1,0:T(4,128)}, u32[]{:S(2)}) copy-start(f32[2,128,2,4,128]{4,3,2,1,0:T(4,128)} %param.20) | copy-start | bytes 3145732
  169.6 9.2 %copy-start.19 = (s32[2,4,128]{2,1,0:T(4,128)S(1)}, s32[2,4,128]{2,1,0:T(4,128)}, u32[]{:S(2)}) copy-start(s32[2,4,128]{2,1,0:T(4,128)} %param.25) | copy-start | bytes 12292
  169.6 9.2 %copy-start.20 = (s32[2,4,128]{2,1,0:T(4,128)S(1)}, s32[2,4,128]{2,1,0:T(4,128)}, u32[]{:S(2)}) copy-start(s32[2,4,128]{2,1,0:T(4,128)} %param.23) | copy-start | bytes 12292
  169.6 14.7 %copy-start.13 = (f32[2,4,128]{2,1,0:T(4,128)S(1)}, f32[2,4,128]{2,1,0:T(4,128)}, u32[]{:S(2)}) copy-start(f32[2,4,128]{2,1,0:T(4,128)} %param.24) | copy-start | bytes 12292
  169.6 14.7 %copy-start.14 = (f32[2,4,128]{2,1,0:T(4,128)S(1)}, f32[2,4,128]{2,1,0:T(4,128)}, u32[]{:S(2)}) copy-start(f32[2,4,128]{2,1,0:T(4,128)} %param.22) | copy-start | bytes 12292
  173.6 13.0 %copy-start = (bf16[8,16,16,512]{3,2,1,0:T(8,128)(2,1)S(1)}, bf16[8,16,16,512]{3,2,1,0:T(8,128)(2,1)}, u32[]{:S(2)}) copy-start(bf16[8,16,16,512]{3,2,1,0:T(8,128)(2,1)} %convert_element_type.318) | copy-start | bytes 6291460
  173.7 10.6 %collective-permute-start = (bf16[2,128,1,4,128]{4,3,2,1,0:T(4,128)(2,1)S(1)}, bf16[2,128,1,4,128]{4,3,2,1,0:T(4,128)(2,1)S(1)}, u32[]{:S(2)}, u32[]{:S(2)}) collective-permute-start(bf16[2,128,1,4,128]{4,3,2,1,0:T(4,128)(2,1)S(1)} %slice.447), channel_id=1, source_target_pairs={{0,2},{2,4},{4,6},{6,8},{8,10},{10,12},{12,14},{14,16},{16,18},{18... | collective-permute-start | bytes 786440 | tf_op jit(solution)/shard_map/ppermute | solution.py:20
  185.4 9.8 %collective-permute-start.1 = (bf16[2,128,1,4,128]{4,3,2,1,0:T(4,128)(2,1)S(1)}, bf16[2,128,1,4,128]{4,3,2,1,0:T(4,128)(2,1)S(1)}, u32[]{:S(2)}, u32[]{:S(2)}) collective-permute-start(bf16[2,128,1,4,128]{4,3,2,1,0:T(4,128)(2,1)S(1)} %slice.446), channel_id=1, source_target_pairs={{2,0},{4,2},{6,4},{8,6},{10,8},{12,10},{14,12},{16,14},{18,16},{20... | collective-permute-start | bytes 786440 | tf_op jit(solution)/shard_map/ppermute | solution.py:20
  196.1 8.4 %collective-permute-start.2 = (bf16[2,128,1,4,128]{4,3,2,1,0:T(4,128)(2,1)S(1)}, bf16[2,128,1,4,128]{4,3,2,1,0:T(4,128)(2,1)S(1)}, u32[]{:S(2)}, u32[]{:S(2)}) collective-permute-start(bf16[2,128,1,4,128]{4,3,2,1,0:T(4,128)(2,1)S(1)} %slice.445), channel_id=1, source_target_pairs={{0,2},{2,4},{4,6},{6,8},{8,10},{10,12},{12,14},{14,16},{16,18},{18... | collective-permute-start | bytes 786440 | tf_op jit(solution)/shard_map/ppermute | solution.py:20
  206.3 24.9 %collective-permute-start.3 = (bf16[2,128,1,4,128]{4,3,2,1,0:T(4,128)(2,1)}, bf16[2,128,1,4,128]{4,3,2,1,0:T(4,128)(2,1)}, u32[]{:S(2)}, u32[]{:S(2)}) collective-permute-start(bf16[2,128,1,4,128]{4,3,2,1,0:T(4,128)(2,1)} %slice.444), channel_id=1, source_target_pairs={{2,0},{4,2},{6,4},{8,6},{10,8},{12,10},{14,12},{16,14},{18,16},{20... | collective-permute-start | bytes 786440 | tf_op jit(solution)/shard_map/ppermute | solution.py:20
  228.7 3.5 %copy-start.11 = (bf16[2,128,2,4,128]{4,3,2,1,0:T(4,128)(2,1)S(1)}, bf16[2,128,2,4,128]{4,3,2,1,0:T(4,128)(2,1)}, u32[]{:S(2)}) copy-start(bf16[2,128,2,4,128]{4,3,2,1,0:T(4,128)(2,1)} %param.21) | copy-start | bytes 1572868
  232.2 4.5 %copy-start.17 = (pred[128]{0:T(512)(128)(4,1)S(1)}, pred[128]{0:T(512)(128)(4,1)}, u32[]{:S(2)}) copy-start(pred[128]{0:T(512)(128)(4,1)} %copy-done.16) | copy-start | bytes 388
  269.5 18.7 %copy-start.2 = (f32[2,128,2,4,128]{4,3,2,1,0:T(4,128)S(1)}, f32[2,128,2,4,128]{4,3,2,1,0:T(4,128)}, u32[]{:S(2)}) copy-start(f32[2,128,2,4,128]{4,3,2,1,0:T(4,128)} %mul.791) | copy-start | bytes 3145732
  269.5 18.7 %copy-start.3 = (f32[2,128,2,4,128]{4,3,2,1,0:T(4,128)S(1)}, f32[2,128,2,4,128]{4,3,2,1,0:T(4,128)}, u32[]{:S(2)}) copy-start(f32[2,128,2,4,128]{4,3,2,1,0:T(4,128)} %mul.786) | copy-start | bytes 3145732
  269.5 18.7 %copy-start.4 = (f32[2,128,2,4,128]{4,3,2,1,0:T(4,128)S(1)}, f32[2,128,2,4,128]{4,3,2,1,0:T(4,128)}, u32[]{:S(2)}) copy-start(f32[2,128,2,4,128]{4,3,2,1,0:T(4,128)} %mul.781) | copy-start | bytes 3145732
  269.5 18.7 %copy-start.5 = (f32[2,128,2,4,128]{4,3,2,1,0:T(4,128)S(1)}, f32[2,128,2,4,128]{4,3,2,1,0:T(4,128)}, u32[]{:S(2)}) copy-start(f32[2,128,2,4,128]{4,3,2,1,0:T(4,128)} %mul.776) | copy-start | bytes 3145732
  269.5 18.7 %copy-start.6 = (f32[2,128,2,4,128]{4,3,2,1,0:T(4,128)S(1)}, f32[2,128,2,4,128]{4,3,2,1,0:T(4,128)}, u32[]{:S(2)}) copy-start(f32[2,128,2,4,128]{4,3,2,1,0:T(4,128)} %mul.771) | copy-start | bytes 3145732
  269.5 18.7 %copy-start.7 = (f32[2,128,2,4,128]{4,3,2,1,0:T(4,128)S(1)}, f32[2,128,2,4,128]{4,3,2,1,0:T(4,128)}, u32[]{:S(2)}) copy-start(f32[2,128,2,4,128]{4,3,2,1,0:T(4,128)} %mul.766) | copy-start | bytes 3145732
  269.5 18.7 %copy-start.8 = (f32[2,128,2,4,128]{4,3,2,1,0:T(4,128)S(1)}, f32[2,128,2,4,128]{4,3,2,1,0:T(4,128)}, u32[]{:S(2)}) copy-start(f32[2,128,2,4,128]{4,3,2,1,0:T(4,128)} %mul.761) | copy-start | bytes 3145732
  269.5 18.7 %copy-start.9 = (f32[2,128,2,4,128]{4,3,2,1,0:T(4,128)S(1)}, f32[2,128,2,4,128]{4,3,2,1,0:T(4,128)}, u32[]{:S(2)}) copy-start(f32[2,128,2,4,128]{4,3,2,1,0:T(4,128)} %mul.756) | copy-start | bytes 3145732
  269.5 18.7 %copy-start.10 = (f32[2,128,2,4,128]{4,3,2,1,0:T(4,128)S(1)}, f32[2,128,2,4,128]{4,3,2,1,0:T(4,128)}, u32[]{:S(2)}) copy-start(f32[2,128,2,4,128]{4,3,2,1,0:T(4,128)} %mul.751) | copy-start | bytes 3145732
  288.3 7.1 %copy-start.18 = (pred[128]{0:T(512)(128)(4,1)S(1)}, pred[128]{0:T(512)(128)(4,1)}, u32[]{:S(2)}) copy-start(pred[128]{0:T(512)(128)(4,1)} %get-tuple-element.171) | copy-start | bytes 388
Sparse Core Ops, SparseCore 0:
  173.7 16.3 all-gather.1
where the time goes:
time: 352 us; the launch traced here: 350 us
  other arithmetic  204 us (58%)
  local copies, waits for them, and re-layouts  61.1 us (17%)
  blocking collectives  44.4 us (13%)
  between operations  14.8 us (4%)
  starting transfers between devices  12.4 us (4%)
  waiting for transfers between devices  12.3 us (3%)
    select_n x16, other arithmetic, eliminate(): jnp.where((positions == pivot_index)[None, :, None, None], pivot_row[:, N...  85.5 us
    psum x1, blocking collectives, shards(): lax.psum((row_table, partial_conc), ('cols', 'params'))  44.4 us
    mul x16, other arithmetic, eliminate(): -column[:, :, None, :] * pivot[:, None, None, :]  32.7 us
    mul x49, local copies, waits for them, and re-layouts, apply_blocks(): factors[:, :, column_index, :].astype(jnp.float32)[None]  31.5 us
    convert_element_type x2, other arithmetic, apply_blocks(): factors[:, :, column_index, :].astype(jnp.float32)[None]  23.1 us
    unnamed x77, local copies, waits for them, and re-layouts  17.2 us
    broadcast_in_dim x16, other arithmetic, eliminate(): jnp.where((positions == pivot_index)[None, :, None, None], pivot_row[:, N...  16.8 us
    div x16, other arithmetic, eliminate(): pivot = 1.0 / current[:, pivot_index, pivot_index, :]  14.9 us
  transfers between devices with their start and end apart: 5, of which 3 were waited for; matrix products, arithmetic and copies ran while one was open for 20% of the time, Pallas kernels for 0%

commit v1 on v0

v1 whole, which is shorter than its diff:
```python
import functools
import jax
import jax.numpy as jnp
from jax import lax
from jax.experimental import pallas as pl
from jax.experimental.pallas import tpu as pltpu
from jax.sharding import PartitionSpec as P

MESH = pl.DeviceIdType.MESH
SUB = 8


def one_hot(column_ref):
    species = column_ref.shape[0]
    at = lax.broadcasted_iota(jnp.int32, (species, species), 1)
    return jnp.where(at == column_ref[...], 1.0, 0.0).astype(jnp.float32)


def exact_dot(left, right, over):
    return lax.dot_general(
        left, right, (over, ((), ())),
        precision=lax.Precision.HIGHEST, preferred_element_type=jnp.float32,
    )


def order_kernel(order_ref, column_ref, conc_ref, emis_ref, sens_ref, src_ref, conc_o, emis_o, sens_o, src_o):
    turn = one_hot(column_ref)
    conc_o[...] = exact_dot(turn, conc_ref[...], ((1,), (0,)))
    emis_o[...] = exact_dot(turn, emis_ref[...], ((1,), (0,)))

    @pl.loop(0, sens_ref.shape[1], unroll=8)
    def _(k):
        at = order_ref[k]
        for g in range(2):
            sens_o[g, k] = sens_ref[g, at]
            src_o[g, k] = src_ref[g, at]


def restore_kernel(order_ref, column_ref, newc_o, news_o, burd_o, newc_ref, news_ref, sburd_ref, cburd_ref):
    turn = one_hot(column_ref)
    newc_ref[...] = exact_dot(turn, newc_o[...], ((0,), (0,)))
    total = exact_dot(burd_o[...], turn, ((1,), (0,)))
    sburd_ref[...] = total[:2]
    cburd_ref[...] = total[2:3]

    @pl.loop(0, news_o.shape[1], unroll=8)
    def _(k):
        at = order_ref[k]
        for g in range(2):
            news_ref[g, at] = news_o[g, k]


def step_kernel(
    ncol, npar, blocks, width, total_cells,
    rate_ref, conc_ref, emis_ref, sens_ref, src_ref, cx_ref, ux_ref, cy_ref, uy_ref,
    newc_ref, news_ref, burd_ref,
    conc_in, conc_rows, emis_rows, newc_rows, invc, lu, mid, coef,
    send1, send2, halo1, halo2, part, cpart, cpart_in, tot_out, tot_in,
    face_c, face_u, conc_ssem, conc_rsem, f_ssem, f_rsem, h_ssem, h_rsem, cp_ssem, cp_rsem, t_ssem, t_rsem,
):
    species = blocks * width
    pairs = width // 2
    half = SUB // 2
    col, par = (lax.axis_index("cols"), lax.axis_index("params"))
    rows = conc_ref.shape[1] // 128
    has_left, has_right = (col > 0, col < ncol - 1)

    barrier = pltpu.get_barrier_semaphore()
    for d in range(1, ncol):
        pl.semaphore_signal(barrier, inc=1, device_id=(lax.rem(col + d, ncol), par), device_id_type=MESH)
    for d in range(1, npar):
        pl.semaphore_signal(barrier, inc=1, device_id=(col, lax.rem(par + d, npar)), device_id_type=MESH)

    row = lax.broadcasted_iota(jnp.int32, (SUB, 128), 0)
    lane = lax.broadcasted_iota(jnp.int32, (SUB, 128), 1)
    top = row < half

    @pl.when(jnp.logical_not(has_left))
    def _():
        halo1[0] = jnp.zeros_like(halo1[0])
        halo2[0] = jnp.zeros_like(halo2[0])

    @pl.when(jnp.logical_not(has_right))
    def _():
        halo1[1] = jnp.zeros_like(halo1[1])
        halo2[1] = jnp.zeros_like(halo2[1])
        face_c[...] = jnp.zeros_like(face_c)
        face_u[...] = jnp.zeros_like(face_u)

    def face_copies():
        def one(src, dst, at):
            return pltpu.make_async_remote_copy(
                src_ref=src, dst_ref=dst, send_sem=f_ssem.at[at], recv_sem=f_rsem.at[at],
                device_id=(jnp.maximum(col - 1, 0), par), device_id_type=MESH,
            )

        return (one(cx_ref, face_c, 0), one(ux_ref, face_u, 1))

    def set_coefficients():
        @pl.when(has_right)
        def _():
            for copy in face_copies():
                copy.wait_recv()

        cx, cy = (cx_ref[...], cy_ref[...])
        ux, uy = (ux_ref[...] == 1, uy_ref[...] == 1)
        zero = jnp.zeros_like(cx)
        in_x, out_x = (jnp.where(ux, cx, zero), jnp.where(ux, zero, cx))
        in_y, out_y = (jnp.where(uy, cy, zero), jnp.where(uy, zero, cy))
        face = pltpu.roll(face_c[...], half, 0)
        up = pltpu.roll(face_u[...], half, 0) == 1
        in_x_face, out_x_face = (jnp.where(up, face, zero), jnp.where(up, zero, face))
        next_in_x = jnp.where(top, pltpu.roll(in_x, half, 0), in_x_face)
        next_out_x = jnp.where(top, pltpu.roll(out_x, half, 0), out_x_face)
        last = lane == 127
        next_in_y = jnp.where(last, zero, pltpu.roll(in_y, 127, 1))
        next_out_y = jnp.where(last, zero, pltpu.roll(out_y, 127, 1))
        coef[0] = 1.0 - (out_x + next_in_x) - (out_y + next_in_y)
        coef[1] = jnp.where(jnp.logical_and(top, jnp.logical_not(has_left)), zero, in_x)
        coef[2] = next_out_x
        coef[3] = jnp.where(lane == 0, zero, in_y)
        coef[4] = next_out_y

    def pack_pair(send, b, k, first, second):
        turned = [pltpu.roll(value, half, 0) for value in first]
        ahead = [jnp.where(top, turned[g], second[g]) for g in range(2)]
        behind = [jnp.where(top, second[g], turned[g]) for g in range(2)]
        send[0, b, k] = jnp.concatenate(ahead, axis=0).astype(jnp.bfloat16)
        send[1, b, k] = jnp.concatenate(behind, axis=0).astype(jnp.bfloat16)

    def halo_copy(which, way, b):
        send, halo = ((send1, halo1), (send2, halo2))[which]
        target = jnp.minimum(col + 1, ncol - 1) if way == 0 else jnp.maximum(col - 1, 0)
        return pltpu.make_async_remote_copy(
            src_ref=send.at[way, b], dst_ref=halo.at[way, b],
            send_sem=h_ssem.at[which, way, b], recv_sem=h_rsem.at[which, way, b],
            device_id=(target, par), device_id_type=MESH,
        )

    def start_halo(which, b):
        @pl.when(has_right)
        def _():
            halo_copy(which, 0, b).start()

        @pl.when(has_left)
        def _():
            halo_copy(which, 1, b).start()

    def wait_halo(which, b):
        @pl.when(has_left)
        def _():
            halo_copy(which, 0, b).wait_recv()

        @pl.when(has_right)
        def _():
            halo_copy(which, 1, b).wait_recv()

    def halo_pair(halo, b, k):
        from_left = halo[0, b, k].astype(jnp.float32)
        from_right = halo[1, b, k].astype(jnp.float32)
        first, second = ([], [])
        for g in range(2):
            low, high = (from_left[g * SUB:(g + 1) * SUB], from_right[g * SUB:(g + 1) * SUB])
            first.append(jnp.where(top, low, high))
            second.append(pltpu.roll(jnp.where(top, high, low), half, 0))
        return (first, second)

    def advance(s, h):
        a0, al, ar, ad, au = (coef[n] for n in range(5))
        turned = pltpu.roll(s, half, 0)
        before_x = jnp.where(top, h, turned)
        after_x = jnp.where(top, turned, h)
        return (
            a0 * s + al * before_x + ar * after_x
            + ad * pltpu.roll(s, 1, 1) + au * pltpu.roll(s, 127, 1)
        )

    def pack_first(b):
        for k in range(pairs):
            i, j = (b * width + 2 * k, b * width + 2 * k + 1)
            pack_pair(send1, b, k, (sens_ref[0, i], sens_ref[1, i]), (sens_ref[0, j], sens_ref[1, j]))

    pack_first(0)
    pl.semaphore_wait(barrier, ncol - 1 + npar - 1)

    @pl.when(has_left)
    def _():
        for copy in face_copies():
            copy.start()

    conc_copies = []
    for d in range(1, npar):
        copy = pltpu.make_async_remote_copy(
            src_ref=conc_ref, dst_ref=conc_in.at[npar - 1 - d],
            send_sem=conc_ssem.at[d - 1], recv_sem=conc_rsem.at[npar - 1 - d],
            device_id=(col, lax.rem(par + d, npar)), device_id_type=MESH,
        )
        copy.start()
        conc_copies.append(copy)

    @pl.loop(1, blocks)
    def _(b):
        pack_first(b)
        start_halo(0, b - 1)

    def spread(read, target, base):
        @pl.loop(0, species // SUB)
        def _(t):
            for r in range(rows):
                target[pl.ds(t * SUB * SUB + base + r, SUB, stride=SUB), :] = read(t, r)

    def own(ref):
        return lambda t, r: ref[pl.ds(pl.multiple_of(t * SUB, SUB), SUB), r * 128:(r + 1) * 128]

    spread(own(conc_ref), conc_rows, par * rows)
    start_halo(0, blocks - 1)
    spread(own(emis_ref), emis_rows, par * rows)
    for d in range(1, npar):
        conc_copies[npar - 1 - d].wait_recv()
        spread(own(conc_in.at[d - 1]), conc_rows, lax.rem(par + d, npar) * rows)

    set_coefficients()

    def tile(ref, index):
        return ref[pl.ds(pl.multiple_of(index * SUB, SUB), SUB), :]

    def factorize(b):
        c = [tile(conc_rows, b * width + j) for j in range(width)]
        for i in range(width):
            invc[b, i] = 1.0 / c[i]

        def fresh(i):
            rates = [rate_ref[b, i * width + j] for j in range(width)]
            total = rates[0] * c[0]
            for j in range(1, width):
                total = total + rates[j] * c[j]
            diagonal = (1.0 + total) * invc[b, i] - rates[i]
            return [diagonal if j == i else jnp.full((SUB, 128), -rates[j], jnp.float32) for j in range(width)]

        for i in range(0, width, 2):
            x, y = (fresh(i), fresh(i + 1))
            for k in range(i):
                inv = lu[b, k, k]
                lx, ly = (x[k] * inv, y[k] * inv)
                lu[b, i, k] = lx
                lu[b, i + 1, k] = ly
                for j in range(k + 1, width):
                    u = lu[b, k, j]
                    x[j] = x[j] - lx * u
                    y[j] = y[j] - ly * u
            inv = 1.0 / x[i]
            lu[b, i, i] = inv
            ly = y[i] * inv
            lu[b, i + 1, i] = ly
            for j in range(i + 1, width):
                lu[b, i, j] = x[j]
                y[j] = y[j] - ly * x[j]
            lu[b, i + 1, i + 1] = 1.0 / y[i + 1]
            for j in range(i + 2, width):
                lu[b, i + 1, j] = y[j]

    def solve(b, sides):
        sides = [list(side) for side in sides]
        for k in range(width):
            for i in range(k + 1, width):
                low = lu[b, i, k]
                for side in sides:
                    side[i] = side[i] - low * side[k]
        for k in range(width - 1, -1, -1):
            inv = lu[b, k, k]
            for side in sides:
                side[k] = side[k] * inv
            for i in range(k):
                up = lu[b, i, k]
                for side in sides:
                    side[i] = side[i] - up * side[k]
        return [[side[k] * invc[b, k] for k in range(width)] for side in sides]

    @pl.loop(0, blocks)
    def _(b):
        factorize(b)
        wait_halo(0, b)
        for k in range(pairs):
            i, j = (b * width + 2 * k, b * width + 2 * k + 1)
            h_first, h_second = halo_pair(halo1, b, k)
            first = [advance(sens_ref[g, i], h_first[g]) for g in range(2)]
            second = [advance(sens_ref[g, j], h_second[g]) for g in range(2)]
            for g in range(2):
                mid[g, b, 2 * k] = first[g]
                mid[g, b, 2 * k + 1] = second[g]
            pack_pair(send2, b, k, first, second)
        base = []
        for k in range(width):
            o = b * width + k
            base.append(tile(conc_rows, o) + tile(emis_rows, o))
        (base,) = solve(b, [base])
        for k in range(width):
            o = b * width + k
            newc_rows[pl.ds(pl.multiple_of(o * SUB, SUB), SUB), :] = base[k]
        start_halo(1, b)

    @pl.loop(0, species // SUB)
    def _(t):
        total = jnp.zeros((SUB, 128), jnp.float32)
        at = pl.ds(pl.multiple_of(t * SUB, SUB), SUB)
        for r in range(rows):
            value = newc_rows[pl.ds(t * SUB * SUB + par * rows + r, SUB, stride=SUB), :]
            newc_ref[at, r * 128:(r + 1) * 128] = value
            total = total + value
        part[0, at, :] = total

    ones = jnp.ones((SUB, 128), jnp.float32)

    def lane_sums(value):
        return lax.dot_general(
            ones, value, (((1,), (1,)), ((), ())),
            precision=lax.Precision.HIGHEST, preferred_element_type=jnp.float32,
        )

    own_c = lane_sums(part[0])
    cpart[...] = own_c
    cpart_in[par] = own_c

    def second_half(b):
        wait_halo(1, b)
        sides = [[], []]
        for k in range(pairs):
            i, j = (b * width + 2 * k, b * width + 2 * k + 1)
            h_first, h_second = halo_pair(halo2, b, k)
            for g in range(2):
                sides[g].append(advance(mid[g, b, 2 * k], h_first[g]) + src_ref[g, i].astype(jnp.float32))
                sides[g].append(advance(mid[g, b, 2 * k + 1], h_second[g]) + src_ref[g, j].astype(jnp.float32))
        sides = solve(b, sides)
        for g in range(2):
            for k in range(width):
                at = (g * species + b * width + k) * SUB
                news_ref[pl.ds(pl.multiple_of(at, SUB), SUB), :] = sides[g][k]

    def cpart_copy(d):
        return pltpu.make_async_remote_copy(
            src_ref=cpart, dst_ref=cpart_in.at[par],
            send_sem=cp_ssem.at[d - 1], recv_sem=cp_rsem.at[d - 1],
            device_id=(col, lax.rem(par + d, npar)), device_id_type=MESH,
        )

    @pl.loop(0, blocks)
    def _(b):
        second_half(b)

        @pl.when(b == 0)
        def _():
            for d in range(1, npar):
                cpart_copy(d).start()

    @pl.loop(0, species // SUB)
    def _(t):
        at = pl.ds(pl.multiple_of(t * SUB, SUB), SUB)
        for g in range(2):
            total = jnp.zeros((SUB, 128), jnp.float32)
            for r in range(SUB):
                total = total + news_ref[pl.ds(g * species * SUB + t * SUB * SUB + r, SUB, stride=SUB), :]
            part[1 + g, at, :] = total

    for d in range(1, npar):
        cpart_copy(d).wait()
    c_total = cpart_in[0]
    for q in range(1, npar):
        c_total = c_total + cpart_in[q]
    sums = [lane_sums(part[1 + g]) for g in range(2)]
    result = jnp.where(row == 0, sums[0], jnp.where(row == 1, sums[1], c_total))
    tot_out[...] = result
    tot_in[col] = result
    for d in range(1, npar):
        conc_copies[d - 1].wait_send()

    @pl.when(has_left)
    def _():
        for copy in face_copies():
            copy.wait_send()

    @pl.loop(0, blocks)
    def _(b):
        for which in range(2):
            @pl.when(has_right)
            def _():
                halo_copy(which, 0, b).wait_send()

            @pl.when(has_left)
            def _():
                halo_copy(which, 1, b).wait_send()

    totals = []
    for d in range(1, ncol):
        copy = pltpu.make_async_remote_copy(
            src_ref=tot_out, dst_ref=tot_in.at[col],
            send_sem=t_ssem.at[d - 1], recv_sem=t_rsem.at[d - 1],
            device_id=(lax.rem(col + d, ncol), par), device_id_type=MESH,
        )
        copy.start()
        totals.append(copy)
    for copy in totals:
        copy.wait()
    total = tot_in[0]
    for q in range(1, ncol):
        total = total + tot_in[q]
    total = total / total_cells
    burd_ref[...] = total


def shards(
    concentration, emissions, rate_table, species_order, sensitivity, source_terms,
    courant_x, upwind_x, courant_y, upwind_y,
):
    ncol, npar = (lax.axis_size("cols"), lax.axis_size("params"))
    blocks, width = (rate_table.shape[0], rate_table.shape[1])
    groups, species, planes, layers, across = sensitivity.shape
    tall = planes * layers
    assert groups == 2 and tall == SUB and planes == 2 and across == 128
    cells = tall * across
    pairs = width // 2

    vm = pltpu.VMEM
    dma = pltpu.SemaphoreType.DMA
    rows_shape = (species * SUB, 128)
    packed_shape = (2, blocks, pairs, 2 * SUB, 128)
    in_vmem = pl.BlockSpec(memory_space=pltpu.VMEM)
    in_smem = pl.BlockSpec(memory_space=pltpu.SMEM)
    order_column = species_order.reshape(species, 1)
    limits = pltpu.CompilerParams(vmem_limit_bytes=16 * 1024 * 1024)
    stacked = (groups, species, SUB, across)
    conc_o, emis_o, sens_o, src_o = pl.pallas_call(
        order_kernel,
        out_shape=(
            jax.ShapeDtypeStruct(concentration.shape, jnp.float32),
            jax.ShapeDtypeStruct(concentration.shape, jnp.float32),
            jax.ShapeDtypeStruct(stacked, jnp.float32),
            jax.ShapeDtypeStruct(stacked, jnp.bfloat16),
        ),
        in_specs=[in_smem] + [in_vmem] * 5,
        out_specs=[in_vmem] * 4,
        compiler_params=limits,
    )(
        species_order, order_column, concentration, emissions,
        sensitivity.reshape(stacked), source_terms.reshape(stacked),
    )
    newc_o, news_o, burd_o = pl.pallas_call(
        functools.partial(step_kernel, ncol, npar, blocks, width, cells * ncol),
        out_shape=(
            jax.ShapeDtypeStruct(concentration.shape, jnp.float32),
            jax.ShapeDtypeStruct((groups * species * SUB, 128), jnp.float32),
            jax.ShapeDtypeStruct((SUB, species), jnp.float32),
        ),
        in_specs=[in_smem] + [in_vmem] * 8,
        out_specs=[in_vmem] * 3,
        scratch_shapes=[
            vm((npar - 1,) + concentration.shape, jnp.float32),
            vm(rows_shape, jnp.float32),
            vm(rows_shape, jnp.float32),
            vm(rows_shape, jnp.float32),
            vm((blocks, width, SUB, 128), jnp.float32),
            vm((blocks, width, width, SUB, 128), jnp.float32),
            vm((groups, blocks, width, SUB, 128), jnp.float32),
            vm((5, SUB, 128), jnp.float32),
            vm(packed_shape, jnp.bfloat16),
            vm(packed_shape, jnp.bfloat16),
            vm(packed_shape, jnp.bfloat16),
            vm(packed_shape, jnp.bfloat16),
            vm((3, species, 128), jnp.float32),
            vm((SUB, species), jnp.float32),
            vm((npar, SUB, species), jnp.float32),
            vm((SUB, species), jnp.float32),
            vm((ncol, SUB, species), jnp.float32),
            vm((SUB, 128), jnp.float32),
            vm((SUB, 128), jnp.int32),
            dma((npar - 1,)), dma((npar - 1,)),
            dma((2,)), dma((2,)),
            dma((2, 2, blocks)), dma((2, 2, blocks)),
            dma((npar - 1,)), dma((npar - 1,)),
            dma((ncol - 1,)), dma((ncol - 1,)),
        ],
        compiler_params=pltpu.CompilerParams(
            collective_id=0, has_side_effects=True, vmem_limit_bytes=48 * 1024 * 1024
        ),
    )(
        rate_table.reshape(blocks, width * width), conc_o, emis_o, sens_o, src_o,
        courant_x.reshape(SUB, across), upwind_x.reshape(SUB, across),
        courant_y.reshape(SUB, across), upwind_y.reshape(SUB, across),
    )
    newc, news, sburd, cburd = pl.pallas_call(
        restore_kernel,
        out_shape=(
            jax.ShapeDtypeStruct(concentration.shape, jnp.float32),
            jax.ShapeDtypeStruct(stacked, jnp.float32),
            jax.ShapeDtypeStruct((groups, species), jnp.float32),
            jax.ShapeDtypeStruct((1, species), jnp.float32),
        ),
        in_specs=[in_smem] + [in_vmem] * 4,
        out_specs=[in_vmem] * 4,
        compiler_params=limits,
    )(species_order, order_column, newc_o, news_o.reshape(stacked), burd_o)
    return (newc, news.reshape(sensitivity.shape), sburd, cburd.reshape(species))


def solution(mesh):
    in_specs = (
        P(None, ("cols", "params")),
        P(None, ("cols", "params")),
        P(),
        P(),
        P("params", None, "cols", None, None),
        P("params", None, "cols", None, None),
        P("cols", None, None),
        P("cols", None, None),
        P("cols", None, None),
        P("cols", None, None),
    )
    out_specs = (
        P(None, ("cols", "params")),
        P("params", None, "cols", None, None),
        P("params", None),
        P(),
    )
    return jax.shard_map(shards, mesh=mesh, in_specs=in_specs, out_specs=out_specs, check_vma=False)
```

time: 352 us -> 48 us (0.14)
  other arithmetic: 204 us -> 0 us
  local copies, waits for them, and re-layouts: 61.1 us -> 5.87 us
  blocking collectives: 44.4 us -> 0 us
  Pallas kernels: 0 us -> 41 us
  between operations: 14.8 us -> 0.71 us
  starting transfers between devices: 12.4 us -> 0 us
  waiting for transfers between devices: 12.3 us -> 0 us
    select_n x20 -> x0, other arithmetic: 86.6 us -> none  [the longest x16 85.5 us: eliminate(): jnp.where((positions == pivot_index)[None, :, None, None], pivot_row[:, N...]
    psum x1 -> x0, blocking collectives: 44.4 us -> none  [shards(): lax.psum((row_table, partial_conc), ('cols', 'params'))]
    pallas_call x0 -> x3, Pallas kernels: none -> 41 us  [the longest x1 37.2 us: shards(): pl.pallas_call(functools.partial(step_kernel, ncol, npar, blocks, width,...]
    mul x18 -> x0, other arithmetic: 34.5 us -> none  [the longest x16 32.7 us: eliminate(): -column[:, :, None, :] * pivot[:, None, None, :]]
    mul x49 -> x0, local copies, waits for them, and re-layouts: 31.5 us -> none  [apply_blocks(): factors[:, :, column_index, :].astype(jnp.float32)[None]]
    convert_element_type x8 -> x0, other arithmetic: 28.1 us -> none  [the longest x2 23.1 us: apply_blocks(): factors[:, :, column_index, :].astype(jnp.float32)[None]]
    broadcast_in_dim x16 -> x0, other arithmetic: 16.8 us -> none  [eliminate(): jnp.where((positions == pivot_index)[None, :, None, None], pivot_row[:, N...]
    div x18 -> x0, other arithmetic: 16 us -> none  [the longest x16 14.9 us: eliminate(): pivot = 1.0 / current[:, pivot_index, pivot_index, :]]
  transfers between devices with their start and end apart: 5 -> 0, of which waited for: 3 -> 0; matrix products, arithmetic and copies ran while one was open for 20% -> 0% of each run, Pallas kernels for 0% -> 0%
where the time goes in v1:
time: 48 us; the launch traced here: 47.6 us
  Pallas kernels  41 us (85%)
  local copies, waits for them, and re-layouts  5.87 us (12%)
  between operations  0.71 us (1%)
    pallas_call x1, Pallas kernels, shards(): pl.pallas_call(functools.partial(step_kernel, ncol, npar, blocks, width,...  37.2 us
    unnamed x18, local copies, waits for them, and re-layouts  4.83 us
    pallas_call x1, Pallas kernels, shards(): pl.pallas_call(restore_kernel, out_shape=(jax.ShapeDtypeStruct(concentrat...  2.34 us
    pallas_call x1, Pallas kernels, shards(): pl.pallas_call(order_kernel, out_shape=(jax.ShapeDtypeStruct(concentratio...  1.5 us

profile of v1, /device:TPU:0, one launch (start us, length us, event | category | flops | bytes accessed | tf_op | source)
XLA Modules:
  0.0 47.6 jit_solution(10328081883322793654)
XLA Ops:
  0.6 0.0 copy-start.4
  0.6 0.9 %reshape.42.rate_ref = f32[8,256]{1,0:T(8,128)S(1)} reshape(f32[8,16,16]{2,1,0:T(8,128)} %param.12) | data formatting | bytes 16384 | tf_op jit(solution)/shard_map/reshape | solution.py:485
  1.6 0.0 copy-done.4
  1.6 0.1 copy.15.column_ref
  1.7 0.0 copy-start
  1.7 1.2 %copy-done = f32[2,128,2,4,128]{4,3,2,1,0:T(4,128)S(1)} copy-done((f32[2,128,2,4,128]{4,3,2,1,0:T(4,128)S(1)}, f32[2,128,2,4,128]{4,3,2,1,0:T(4,128)}, u32[]{:S(2)}) %copy-start) | copy-done | bytes 1048600
  2.9 0.0 copy-start.1
  2.9 1.0 %copy-done.1 = bf16[2,128,2,4,128]{4,3,2,1,0:T(4,128)(2,1)S(1)} copy-done((bf16[2,128,2,4,128]{4,3,2,1,0:T(4,128)(2,1)S(1)}, bf16[2,128,2,4,128]{4,3,2,1,0:T(4,128)(2,1)}, u32[]{:S(2)}) %copy-start.1) | copy-done | bytes 524312
  4.0 0.0 copy-start.2
  4.0 0.9 %copy-done.2 = f32[128,512]{1,0:T(8,128)S(1)} copy-done((f32[128,512]{1,0:T(8,128)S(1)}, f32[128,512]{1,0:T(8,128)}, u32[]{:S(2)}) %copy-start.2) | copy-done | bytes 262168
  4.9 0.0 copy-start.3
  4.9 0.9 %copy-done.3 = f32[128,512]{1,0:T(8,128)S(1)} copy-done((f32[128,512]{1,0:T(8,128)S(1)}, f32[128,512]{1,0:T(8,128)}, u32[]{:S(2)}) %copy-start.3) | copy-done | bytes 262168
  5.9 0.0 copy-start.6
  5.9 0.0 copy-start.7
  5.9 0.0 copy-start.8
  5.9 1.5 %shard_map.129 = (f32[128,512]{1,0:T(8,128)S(1)}, f32[128,512]{1,0:T(8,128)S(1)}, f32[2,128,8,128]{3,2,1,0:T(8,128)S(1)}, bf16[2,128,8,128]{3,2,1,0:T(8,128)(2,1)S(1)}) custom-call(s32[128]{0:T(128)S(1)} %copy-done.4, s32[128,1]{1,0:T(8,128)S(1)} %copy.15.column_ref, f32[128,512]{1,0:T(8,128)S(1)} %copy-done.2, f32[128,512]{1,0:T(8,128)S(1)} %copy-done.3, ...), custom_call_target="tpu_custom_call" | custom-call | tf_op jit(solution)/shard_map/pallas_call | solution.py:431
  7.4 0.0 copy-start.5
  7.4 0.0 copy-done.6
  7.4 0.0 copy-done.7
  7.4 0.0 copy-done.8
  7.4 0.6 %copy-done.5 = f32[2,4,128]{2,1,0:T(4,128)S(1)} copy-done((f32[2,4,128]{2,1,0:T(4,128)S(1)}, f32[2,4,128]{2,1,0:T(4,128)}, u32[]{:S(2)}) %copy-start.5) | copy-done | bytes 4120
  8.1 37.2 %shard_map.130 = (f32[128,512]{1,0:T(8,128)S(1)}, f32[2048,128]{1,0:T(8,128)S(1)}, f32[8,128]{1,0:T(8,128)S(1)}) custom-call(f32[8,256]{1,0:T(8,128)S(1)} %reshape.42.rate_ref, f32[128,512]{1,0:T(8,128)S(1)} %get-tuple-element.15.conc_ref, f32[128,512]{1,0:T(8,128)S(1)} %get-tuple-element.16.emis_ref, f32[2,128,8,128]{3,2,1,0:T(8,128)S(1)} %get-tuple-element.17.sens_ref, ...), custom_call_target="tpu_custom_call" | custom-call | tf_op jit(solution)/shard_map/pallas_call | solution.py:446
  45.3 2.3 %shard_map.131 = (f32[128,512]{1,0:T(8,128)}, f32[2,128,8,128]{3,2,1,0:T(8,128)}, f32[2,128]{1,0:T(2,128)}, f32[1,128]{1,0:T(1,128)}) custom-call(s32[128]{0:T(128)S(1)} %copy-done.4, s32[128,1]{1,0:T(8,128)S(1)} %copy.15.column_ref, f32[128,512]{1,0:T(8,128)S(1)} %get-tuple-element.19.newc_o, f32[2,128,8,128]{3,2,1,0:T(8,128)S(1)} %bitcast.11, ...), custom_call_target="tpu_custom_call" | custom-call | tf_op jit(solution)/shard_map/pallas_call | solution.py:489
Async XLA Ops:
  0.6 0.9 %copy-start.4 = (s32[128]{0:T(128)S(1)}, s32[128]{0:T(128)}, u32[]{:S(2)}) copy-start(s32[128]{0:T(128)} %order_ref.3) | copy-start | bytes 1540
  1.7 1.2 %copy-start = (f32[2,128,2,4,128]{4,3,2,1,0:T(4,128)S(1)}, f32[2,128,2,4,128]{4,3,2,1,0:T(4,128)}, u32[]{:S(2)}) copy-start(f32[2,128,2,4,128]{4,3,2,1,0:T(4,128)} %param.14) | copy-start | bytes 3145732
  2.9 1.0 %copy-start.1 = (bf16[2,128,2,4,128]{4,3,2,1,0:T(4,128)(2,1)S(1)}, bf16[2,128,2,4,128]{4,3,2,1,0:T(4,128)(2,1)}, u32[]{:S(2)}) copy-start(bf16[2,128,2,4,128]{4,3,2,1,0:T(4,128)(2,1)} %param.15) | copy-start | bytes 1572868
  4.0 0.9 %copy-start.2 = (f32[128,512]{1,0:T(8,128)S(1)}, f32[128,512]{1,0:T(8,128)}, u32[]{:S(2)}) copy-start(f32[128,512]{1,0:T(8,128)} %conc_ref.1) | copy-start | bytes 786436
  4.9 0.9 %copy-start.3 = (f32[128,512]{1,0:T(8,128)S(1)}, f32[128,512]{1,0:T(8,128)}, u32[]{:S(2)}) copy-start(f32[128,512]{1,0:T(8,128)} %emis_ref.1) | copy-start | bytes 786436
  5.9 1.5 %copy-start.6 = (s32[2,4,128]{2,1,0:T(4,128)S(1)}, s32[2,4,128]{2,1,0:T(4,128)}, u32[]{:S(2)}) copy-start(s32[2,4,128]{2,1,0:T(4,128)} %param.17) | copy-start | bytes 12292
  5.9 1.5 %copy-start.7 = (f32[2,4,128]{2,1,0:T(4,128)S(1)}, f32[2,4,128]{2,1,0:T(4,128)}, u32[]{:S(2)}) copy-start(f32[2,4,128]{2,1,0:T(4,128)} %param.18) | copy-start | bytes 12292
  5.9 1.5 %copy-start.8 = (s32[2,4,128]{2,1,0:T(4,128)S(1)}, s32[2,4,128]{2,1,0:T(4,128)}, u32[]{:S(2)}) copy-start(s32[2,4,128]{2,1,0:T(4,128)} %param.19) | copy-start | bytes 12292
  7.4 0.7 %copy-start.5 = (f32[2,4,128]{2,1,0:T(4,128)S(1)}, f32[2,4,128]{2,1,0:T(4,128)}, u32[]{:S(2)}) copy-start(f32[2,4,128]{2,1,0:T(4,128)} %param.16) | copy-start | bytes 12292

commit v2 on v1

--- a/solution.py
+++ b/solution.py
@@ -10,6 +10,10 @@
 SUB = 8
 
 
+def pinned(value):
+    return pltpu.with_memory_space_constraint(value, pltpu.HBM)
+
+
 def one_hot(column_ref):
     species = column_ref.shape[0]
     at = lax.broadcasted_iota(jnp.int32, (species, species), 1)
@@ -23,10 +27,18 @@
     )
 
 
-def order_kernel(order_ref, column_ref, conc_ref, emis_ref, sens_ref, src_ref, conc_o, emis_o, sens_o, src_o):
+def order_kernel(order_ref, column_ref, conc_hbm, emis_hbm, sens_hbm, src_hbm, conc_o, emis_o, sens_o, src_o, conc_ref, emis_ref, sens_ref, src_ref, sems):
+    held = ((conc_hbm, conc_ref), (emis_hbm, emis_ref), (sens_hbm, sens_ref), (src_hbm, src_ref))
+    copies = [pltpu.make_async_copy(src, dst, sems.at[n]) for n, (src, dst) in enumerate(held)]
+    for copy in copies:
+        copy.start()
     turn = one_hot(column_ref)
+    copies[0].wait()
     conc_o[...] = exact_dot(turn, conc_ref[...], ((1,), (0,)))
+    copies[1].wait()
     emis_o[...] = exact_dot(turn, emis_ref[...], ((1,), (0,)))
+    copies[2].wait()
+    copies[3].wait()
 
     @pl.loop(0, sens_ref.shape[1], unroll=8)
     def _(k):
@@ -436,12 +448,19 @@
             jax.ShapeDtypeStruct(stacked, jnp.float32),
             jax.ShapeDtypeStruct(stacked, jnp.bfloat16),
         ),
-        in_specs=[in_smem] + [in_vmem] * 5,
+        in_specs=[in_smem, in_vmem] + [pl.BlockSpec(memory_space=pltpu.HBM)] * 4,
         out_specs=[in_vmem] * 4,
+        scratch_shapes=[
+            vm(concentration.shape, jnp.float32),
+            vm(concentration.shape, jnp.float32),
+            vm(stacked, jnp.float32),
+            vm(stacked, jnp.bfloat16),
+            dma((4,)),
+        ],
         compiler_params=limits,
     )(
-        species_order, order_column, concentration, emissions,
-        sensitivity.reshape(stacked), source_terms.reshape(stacked),
+        species_order, order_column, pinned(concentration), pinned(emissions),
+        pinned(sensitivity.reshape(stacked)), pinned(source_terms.reshape(stacked)),
     )
     newc_o, news_o, burd_o = pl.pallas_call(
         functools.partial(step_kernel, ncol, npar, blocks, width, cells * ncol),

time: 48 us -> 44.8 us (0.933)
  local copies, waits for them, and re-layouts: 5.87 us -> 1.72 us
  Pallas kernels: 41 us -> 42.1 us
    unnamed x18 -> x10, local copies, waits for them, and re-layouts: 4.83 us -> 0.67 us
    pallas_call x1, Pallas kernels: 1.5 us -> 2.6 us  [shards(): pl.pallas_call(order_kernel, out_shape=(jax.ShapeDtypeStruct(concentratio...]
where the time goes in v2:
time: 44.8 us; the launch traced here: 44.6 us
  Pallas kernels  42.1 us (94%)
  local copies, waits for them, and re-layouts  1.72 us (4%)
  between operations  0.72 us (2%)
    pallas_call x1, Pallas kernels, shards(): pl.pallas_call(functools.partial(step_kernel, ncol, npar, blocks, width,...  37.2 us
    pallas_call x1, Pallas kernels, shards(): pl.pallas_call(order_kernel, out_shape=(jax.ShapeDtypeStruct(concentratio...  2.6 us
    pallas_call x1, Pallas kernels, shards(): pl.pallas_call(restore_kernel, out_shape=(jax.ShapeDtypeStruct(concentrat...  2.34 us
    reshape x1, local copies, waits for them, and re-layouts, shards(): rate_table.reshape(blocks, width * width)  0.93 us

profile of v2, /device:TPU:0, one launch (start us, length us, event | category | flops | bytes accessed | tf_op | source)
XLA Modules:
  0.0 44.6 jit_solution(16300522869954916104)
XLA Ops:
  0.6 0.0 copy-start
  0.6 0.9 %reshape.42.rate_ref = f32[8,256]{1,0:T(8,128)S(1)} reshape(f32[8,16,16]{2,1,0:T(8,128)} %param.12) | data formatting | bytes 16384 | tf_op jit(solution)/shard_map/reshape | solution.py:504
  1.6 0.0 copy-done
  1.6 0.1 copy.15.column_ref
  1.7 0.0 copy-start.2
  1.7 0.0 copy-start.3
  1.7 0.0 copy-start.4
  1.7 2.6 %shard_map.129 = (f32[128,512]{1,0:T(8,128)S(1)}, f32[128,512]{1,0:T(8,128)S(1)}, f32[2,128,8,128]{3,2,1,0:T(8,128)S(1)}, bf16[2,128,8,128]{3,2,1,0:T(8,128)(2,1)S(1)}) custom-call(s32[128]{0:T(128)S(1)} %copy-done, s32[128,1]{1,0:T(8,128)S(1)} %copy.15.column_ref, f32[128,512]{1,0:T(8,128)} %conc_hbm.1, f32[128,512]{1,0:T(8,128)} %emis_hbm.1, ...), custom_call_target="tpu_custom_call" | custom-call | tf_op jit(solution)/shard_map/pallas_call | solution.py:443
  4.3 0.0 copy-start.1
  4.3 0.0 copy-done.2
  4.4 0.0 copy-done.3
  4.4 0.0 copy-done.4
  4.4 0.6 %copy-done.1 = f32[2,4,128]{2,1,0:T(4,128)S(1)} copy-done((f32[2,4,128]{2,1,0:T(4,128)S(1)}, f32[2,4,128]{2,1,0:T(4,128)}, u32[]{:S(2)}) %copy-start.1) | copy-done | bytes 4120
  5.0 37.2 %shard_map.130 = (f32[128,512]{1,0:T(8,128)S(1)}, f32[2048,128]{1,0:T(8,128)S(1)}, f32[8,128]{1,0:T(8,128)S(1)}) custom-call(f32[8,256]{1,0:T(8,128)S(1)} %reshape.42.rate_ref, f32[128,512]{1,0:T(8,128)S(1)} %get-tuple-element.15.conc_ref, f32[128,512]{1,0:T(8,128)S(1)} %get-tuple-element.16.emis_ref, f32[2,128,8,128]{3,2,1,0:T(8,128)S(1)} %get-tuple-element.17.sens_ref, ...), custom_call_target="tpu_custom_call" | custom-call | tf_op jit(solution)/shard_map/pallas_call | solution.py:465
  42.2 2.3 %shard_map.131 = (f32[128,512]{1,0:T(8,128)}, f32[2,128,8,128]{3,2,1,0:T(8,128)}, f32[2,128]{1,0:T(2,128)}, f32[1,128]{1,0:T(1,128)}) custom-call(s32[128]{0:T(128)S(1)} %copy-done, s32[128,1]{1,0:T(8,128)S(1)} %copy.15.column_ref, f32[128,512]{1,0:T(8,128)S(1)} %get-tuple-element.19.newc_o, f32[2,128,8,128]{3,2,1,0:T(8,128)S(1)} %bitcast.10, ...), custom_call_target="tpu_custom_call" | custom-call | tf_op jit(solution)/shard_map/pallas_call | solution.py:508
Async XLA Ops:
  0.6 0.9 %copy-start = (s32[128]{0:T(128)S(1)}, s32[128]{0:T(128)}, u32[]{:S(2)}) copy-start(s32[128]{0:T(128)} %order_ref.3) | copy-start | bytes 1540
  1.7 2.6 %copy-start.2 = (s32[2,4,128]{2,1,0:T(4,128)S(1)}, s32[2,4,128]{2,1,0:T(4,128)}, u32[]{:S(2)}) copy-start(s32[2,4,128]{2,1,0:T(4,128)} %param.17) | copy-start | bytes 12292
  1.7 2.7 %copy-start.3 = (f32[2,4,128]{2,1,0:T(4,128)S(1)}, f32[2,4,128]{2,1,0:T(4,128)}, u32[]{:S(2)}) copy-start(f32[2,4,128]{2,1,0:T(4,128)} %param.18) | copy-start | bytes 12292
  1.7 2.6 %copy-start.4 = (s32[2,4,128]{2,1,0:T(4,128)S(1)}, s32[2,4,128]{2,1,0:T(4,128)}, u32[]{:S(2)}) copy-start(s32[2,4,128]{2,1,0:T(4,128)} %param.19) | copy-start | bytes 12292
  4.3 0.7 %copy-start.1 = (f32[2,4,128]{2,1,0:T(4,128)S(1)}, f32[2,4,128]{2,1,0:T(4,128)}, u32[]{:S(2)}) copy-start(f32[2,4,128]{2,1,0:T(4,128)} %param.16) | copy-start | bytes 12292
